TPU v7x, 256 devices: a whole 4x4x8 slice. The times are simulated.
256 devices in a mesh: leaf: 16 (over y, x), sep: 8 (over z), mode: 2 (over core).
Axes of the slice: x: 4, y: 4, z: 8, core: 2. Of those that a mesh axis runs over, the one named last changes fastest.
Arguments:
- modes: bfloat16 [1024, 2048, 256], P(('leaf', 'sep'), 'mode'), may hold values from -0.125 to 0.125
- coupling: bfloat16 [1024, 2048, 256], P(('leaf', 'sep'), 'mode'), may hold values from -6 to 6
- eigenvalues: float32 [1024, 256], P(('leaf', 'sep'), 'mode'), may hold values from 200 to 4000
- separator_of: int32 [1024, 1], P(('leaf', 'sep')), may hold values from 0 to 7; in each aligned block of 8 rows (0 to 7, 8 to 15, ...) at most 2 rows name the same one
- row_offset: int32 [1024], P(('leaf', 'sep')), may hold values from 0 to 256
- stiffness: bfloat16 [8, 512, 512], P('sep', None, ('leaf', 'mode')), may hold values from -1 to 40
- start_block: bfloat16 [8, 512, 256], P('sep', ('leaf', 'mode')), may hold values from -40 to 40
- rotations: bfloat16 [8, 2, 256, 256], P('sep'), may hold values from -0.375 to 0.375
Outputs:
- subspace: bfloat16 [8, 512, 256], P('sep', ('leaf', 'mode'))
- column_norms: float32 [8, 2, 256], P('sep')
Inputs may be any that keep to these rules, and one draw needn't show every extreme that they name: `separator_of`: among the 8 leaves of one device at most 2 couple to one separator, and in every draw some separator gets exactly 2 of them.
All inputs are finite; a program needn't handle non-finite values.
Results may differ from a plain program's by a relative error of at most 0.0075.
Values may be sent and summed in bfloat16 or wider, within the bound.
No kernel may reach another device: no remote copies, remote signals or barrier semaphores. Data moves between devices by JAX's collectives and lax.ppermute only.
A program may use at most 64 MiB of HBM per device.

v0:
```python
import jax
import jax.numpy as jnp
from jax import lax
from jax.sharding import PartitionSpec as P

SEP_ROWS = 512
CAP = 2
ITERS = 2
epsilon = 1e-06


def leaf_projection(modes, coupling, eigenvalues):
    summed = lax.psum_scatter(
        jnp.einsum("ldm,ldw->mlw", modes, coupling, preferred_element_type=jnp.float32),
        "mode",
        scatter_dimension=0,
        tiled=True,
    )
    return (summed / jnp.sqrt(eigenvalues.T)[:, :, None]).astype(jnp.bfloat16)


def route_blocks(scaled, separator_of, row_offset):
    groups = lax.axis_size("sep")
    leaves = scaled.shape[1]
    target = separator_of[:, 0]
    leaf_order = jnp.arange(leaves)
    earlier = (target[:, None] == target[None, :]) & (leaf_order[None, :] < leaf_order[:, None])
    position = jnp.sum(earlier.astype(jnp.int32), 1)
    slot_of = target * CAP + position
    slot_table = slot_of[None, :] == jnp.arange(groups * CAP)[:, None]
    send_blocks = jnp.einsum(
        "sl,mlw->smw", slot_table.astype(jnp.bfloat16), scaled, preferred_element_type=jnp.float32
    ).astype(jnp.bfloat16)
    send_offsets = jnp.sum(jnp.where(slot_table, row_offset[None, :], 0), 1)
    block_shape = (groups, CAP, send_blocks.shape[1], send_blocks.shape[2])
    got_blocks, got_offsets = (
        lax.all_to_all(
            send_blocks.reshape(block_shape), "sep", split_axis=0, concat_axis=0, tiled=True
        ),
        lax.all_to_all(
            send_offsets.reshape(groups, CAP), "sep", split_axis=0, concat_axis=0, tiled=True
        ),
    )
    return (
        got_blocks.reshape(groups * CAP, block_shape[2], block_shape[3]),
        got_offsets.reshape(groups * CAP),
    )


def coupled_correction(full_block, blocks, offsets):
    width_rows = blocks.shape[2]

    def add_slot(slot_index, accumulated):
        offset = offsets[slot_index]
        weights = blocks[slot_index]
        window = lax.dynamic_slice_in_dim(full_block, offset, width_rows, 0)
        projected = jnp.dot(weights, window, preferred_element_type=jnp.float32).astype(
            jnp.bfloat16
        )
        update = jnp.einsum("mw,mc->wc", weights, projected, preferred_element_type=jnp.float32)
        current = lax.dynamic_slice_in_dim(accumulated, offset, width_rows, 0)
        return lax.dynamic_update_slice_in_dim(accumulated, current + update, offset, 0)

    initial = jnp.zeros(full_block.shape, jnp.float32)
    return lax.fori_loop(0, blocks.shape[0], add_slot, initial)


def gather_rows(own_block):
    return lax.all_gather(own_block, ("leaf", "mode"), axis=0, tiled=True)


def per_device(
    modes, coupling, eigenvalues, separator_of, row_offset, stiffness, start_block, rotations
):
    scaled = leaf_projection(modes, coupling, eigenvalues)
    blocks, offsets = route_blocks(scaled, separator_of, row_offset)
    stiff_columns = stiffness[0]
    own_block = start_block[0]
    ritz_turns = rotations[0]
    own_rows = own_block.shape[0]
    norm_list = []
    for iteration in range(ITERS):
        full_block = gather_rows(own_block)
        correction = coupled_correction(full_block, blocks, offsets)

        def assemble_rows(first_row, row_count, block_now=own_block, correction_now=correction):
            product = jnp.dot(stiff_columns, block_now, preferred_element_type=jnp.float32)
            return product - correction_now

        summed = lax.psum_scatter(
            assemble_rows(jnp.int32(0), lax.axis_size(("leaf", "mode")) * own_rows),
            ("leaf", "mode"),
            scatter_dimension=0,
            tiled=True,
        )
        squares = lax.psum(jnp.sum(summed * summed, 0), ("leaf", "mode"))
        column_scale = jnp.sqrt(squares / SEP_ROWS + epsilon)
        normed = (summed / column_scale).astype(jnp.bfloat16)
        own_block = jnp.dot(
            normed, ritz_turns[iteration], preferred_element_type=jnp.float32
        ).astype(jnp.bfloat16)
        norm_list.append(column_scale)
    return (own_block[None], jnp.stack(norm_list)[None])


def solution(mesh):
    in_specs = (
        P(("leaf", "sep"), "mode", None),
        P(("leaf", "sep"), "mode", None),
        P(("leaf", "sep"), "mode"),
        P(("leaf", "sep"), None),
        P(("leaf", "sep")),
        P("sep", None, ("leaf", "mode")),
        P("sep", ("leaf", "mode"), None),
        P("sep", None, None, None),
    )
    out_specs = (P("sep", ("leaf", "mode"), None), P("sep", None, None))
    return jax.shard_map(
        per_device, mesh=mesh, in_specs=in_specs, out_specs=out_specs, check_vma=False
    )
```

profile of v0, /device:TPU:1, one launch (start us, length us, event | category | flops | bytes accessed | tf_op | source)
XLA Modules:
  0.0 560.8 jit_solution(13401757239637969915)
XLA Ops:
  7.3 6.2 %convolution_bitcast_fusion = f32[256,8,256]{0,2,1:T(8,128)} fusion(bf16[8,1024,256]{2,1,0:T(8,128)(2,1)} %param.13, bf16[8,1024,256]{2,1,0:T(8,128)(2,1)} %param.12), kind=kOutput, calls=%fused_computation.13 | convolution fusion | flops 1073741824 | bytes 10485760 | tf_op jit(solution)/shard_map/ldm,ldw->mlw/dot_general | solution.py:14
  14.5 9.0 %all-to-all-start = ((s32[8,1,2]{2,1,0:T(1,128)}), s32[8,1,2]{2,1,0:T(1,128)S(1)}, u32[]{:S(2)}, u32[]{:S(2)}) async-start(s32[8,1,2]{2,1,0:T(1,128)} %bitcast.7), calls=%async_computation | async-start | bytes 8192 | tf_op jit(solution)/shard_map/all_to_all | solution.py:40
  23.5 9.3 %reduce-scatter.6.cloned.1.call-done = f32[128,8,256]{0,2,1:T(8,128)} async-done(((f32[256,8,256]{0,2,1:T(8,128)}), f32[128,8,256]{0,2,1:T(8,128)}) %reduce-scatter.6.cloned.1.call-update) | async-done | bytes 1048592 | tf_op jit(solution)/shard_map/reduce_scatter | solution.py:13
  37.3 6.8 %all-to-all-start.1 = ((bf16[8,2,128,256]{3,1,2,0:T(2,128)(2,1)}), bf16[8,2,128,256]{3,1,2,0:T(2,128)(2,1)S(1)}, u32[]{:S(2)}, u32[]{:S(2)}) async-start(bf16[8,2,128,256]{3,1,2,0:T(2,128)(2,1)} %copy.30), calls=%async_computation.2 | async-start | bytes 2097152 | tf_op jit(solution)/shard_map/all_to_all | solution.py:37
  44.2 25.3 %all-gather = bf16[1,512,256]{2,1,0:T(8,128)(2,1)S(1)} all-gather(bf16[1,16,256]{2,1,0:T(8,128)(2,1)S(1)} %copy-done.1), channel_id=2, replica_groups=mesh['leaf'=16,'sep'=8,'mode'=2] {'leaf','mode'}, dimensions={1}, use_global_device_ids=true | all-gather | bytes 270336 | tf_op jit(solution)/shard_map/all_gather | solution.py:69
  70.8 2.6 all-to-all-done.1
  73.6 74.0 %while.26 = (s32[]{:T(128)}, f32[512,256]{1,0:T(8,128)S(1)}, s32[16]{0:T(128)S(1)}, bf16[16,128,256]{2,1,0:T(8,128)(2,1)S(1)}, bf16[512,256]{1,0:T(8,128)(2,1)S(1)}, /*index=5*/s32[]{:T(128)}, s32[]{:T(128)}, s32[]{:T(128)}) while((s32[]{:T(128)}, f32[512,256]{1,0:T(8,128)S(1)}, s32[16]{0:T(128)S(1)}, bf16[16,128,256]{2,1,0:T(8,128)(2,1)S(1)}, ...), condition=%wide.region_4.5_spmd, body=%wide.region_3.4_spmd.sunk | while | flops 33652740 | bytes 1312903 | solution.py:65
  148.8 80.6 %reduce-scatter.8.cloned.1.call-done = f32[16,256]{1,0:T(8,128)} async-done(((f32[512,256]{1,0:T(8,128)}), f32[16,256]{1,0:T(8,128)}) %reduce-scatter.8.cloned.1.call-update) | async-done | bytes 16400 | tf_op jit(solution)/shard_map/reduce_scatter | solution.py:90
  230.1 64.6 %psum.14 = f32[256]{0:T(256)S(1)} all-reduce(f32[256]{0:T(256)S(1)} %multiply_reduce_fusion.1), channel_id=1, replica_groups=mesh['leaf'=16,'sep'=8,'mode'=2] {'leaf','mode'}, use_global_device_ids=true, to_apply=%region_7.8 | all-reduce | flops 256 | bytes 2048 | tf_op jit(solution)/shard_map/psum | solution.py:96
  295.6 22.6 %all_gather.7 = bf16[512,256]{1,0:T(8,128)(2,1)S(1)} all-gather(bf16[16,256]{1,0:T(8,128)(2,1)S(1)} %convolution_convert_fusion.4), channel_id=1, replica_groups=mesh['leaf'=16,'sep'=8,'mode'=2] {'leaf','mode'}, dimensions={0}, use_global_device_ids=true | all-gather | bytes 270336 | tf_op jit(solution)/shard_map/all_gather | solution.py:69
  318.3 85.1 %while.27 = (s32[]{:T(128)}, f32[512,256]{0,1:T(8,128)S(1)}, s32[16]{0:T(128)S(1)}, bf16[16,128,256]{2,1,0:T(8,128)(2,1)S(1)}, bf16[512,256]{1,0:T(8,128)(2,1)S(1)}, /*index=5*/s32[]{:T(128)}, s32[]{:T(128)}, s32[]{:T(128)}) while((s32[]{:T(128)}, f32[512,256]{0,1:T(8,128)S(1)}, s32[16]{0:T(128)S(1)}, bf16[16,128,256]{2,1,0:T(8,128)(2,1)S(1)}, ...), condition=%wide.region_9.10_spmd, body=%wide.region_8.9_spmd.sunk | while | flops 33652740 | bytes 2884751 | solution.py:65
  326.8 1.9 dynamic_update_slice.17
  332.1 1.9 dynamic_update_slice.17
  337.4 1.9 dynamic_update_slice.17
  347.9 1.9 dynamic_update_slice.17
  353.1 2.2 dynamic_update_slice.17
  358.7 1.9 dynamic_update_slice.17
  369.2 1.9 dynamic_update_slice.17
  374.5 2.2 dynamic_update_slice.17
  390.6 1.9 dynamic_update_slice.17
  395.8 2.2 dynamic_update_slice.17
  401.4 1.9 dynamic_update_slice.17
  404.7 82.7 %reduce-scatter.10.cloned.1.call-done = f32[16,256]{1,0:T(8,128)} async-done(((f32[512,256]{1,0:T(8,128)}), f32[16,256]{1,0:T(8,128)}) %reduce-scatter.10.cloned.1.call-update) | async-done | bytes 16400
  488.2 64.6 %psum.15 = f32[256]{0:T(256)S(1)} all-reduce(f32[256]{0:T(256)S(1)} %multiply_reduce_fusion), channel_id=1, replica_groups=mesh['leaf'=16,'sep'=8,'mode'=2] {'leaf','mode'}, use_global_device_ids=true, to_apply=%region_12.13 | all-reduce | flops 256 | bytes 2048 | tf_op jit(solution)/shard_map/psum | solution.py:96
  (179 shorter events, 86.9 us)
Async XLA Ops:
  7.2 140.5 %copy-start = (bf16[1,512,16]{1,2,0:T(8,128)(2,1)S(1)}, bf16[1,512,16]{1,2,0:T(8,128)(2,1)}, u32[]{:S(2)}) copy-start(bf16[1,512,16]{1,2,0:T(8,128)(2,1)} %param.17) | copy-start | bytes 49156
  7.2 6.3 %copy-start.4 = (s32[8,1]{0,1:T(1,128)S(1)}, s32[8,1]{0,1:T(1,128)}, u32[]{:S(2)}) copy-start(s32[8,1]{0,1:T(1,128)} %param.15) | copy-start | bytes 100
  7.2 6.5 %copy-start.5 = (s32[8]{0:T(128)S(1)}, s32[8]{0:T(128)}, u32[]{:S(2)}) copy-start(s32[8]{0:T(128)} %param.16) | copy-start | bytes 100
  7.2 16.3 %copy-start.2 = (f32[8,128]{1,0:T(8,128)S(1)}, f32[8,128]{1,0:T(8,128)}, u32[]{:S(2)}) copy-start(f32[8,128]{1,0:T(8,128)} %param.14) | copy-start | bytes 12292
  7.2 25.6 %reduce-scatter.6.cloned.1.call-start = ((), (), s32[]{:S(2)}) async-start(), calls=%async_computation.5 | async-start | bytes 3145728 | tf_op jit(solution)/shard_map/reduce_scatter | solution.py:13
  14.5 22.9 %all-to-all-start = ((s32[8,1,2]{2,1,0:T(1,128)}), s32[8,1,2]{2,1,0:T(1,128)S(1)}, u32[]{:S(2)}, u32[]{:S(2)}) async-start(s32[8,1,2]{2,1,0:T(1,128)} %bitcast.7), calls=%async_computation | async-start | bytes 8192 | tf_op jit(solution)/shard_map/all_to_all | solution.py:40
  34.5 9.6 %copy-start.1 = (bf16[1,16,256]{2,1,0:T(8,128)(2,1)S(1)}, bf16[1,16,256]{2,1,0:T(8,128)(2,1)}, u32[]{:S(2)}) copy-start(bf16[1,16,256]{2,1,0:T(8,128)(2,1)} %param.18) | copy-start | bytes 24580
  37.3 36.0 %all-to-all-start.1 = ((bf16[8,2,128,256]{3,1,2,0:T(2,128)(2,1)}), bf16[8,2,128,256]{3,1,2,0:T(2,128)(2,1)S(1)}, u32[]{:S(2)}, u32[]{:S(2)}) async-start(bf16[8,2,128,256]{3,1,2,0:T(2,128)(2,1)} %copy.30), calls=%async_computation.2 | async-start | bytes 2097152 | tf_op jit(solution)/shard_map/all_to_all | solution.py:37
  44.1 185.3 %reduce-scatter.8.cloned.1.call-start = ((), (), s32[]{:S(2)}) async-start(), calls=%async_computation.6 | async-start | bytes 540672 | tf_op jit(solution)/shard_map/reduce_scatter | solution.py:90
  73.6 221.1 %copy-start.3 = (bf16[1,2,256,256]{3,2,1,0:T(8,128)(2,1)S(1)}, bf16[1,2,256,256]{3,2,1,0:T(8,128)(2,1)}, u32[]{:S(2)}) copy-start(bf16[1,2,256,256]{3,2,1,0:T(8,128)(2,1)} %param.19) | copy-start | bytes 786436
  148.7 338.6 %reduce-scatter.10.cloned.1.call-start = ((), (), s32[]{:S(2)}) async-start(), calls=%async_computation.7 | async-start | bytes 540672
Sparse Core Ops, SparseCore 0:
  13.6 19.1 reduce-scatter.5
  148.9 80.5 reduce-scatter.7
  404.8 82.4 reduce-scatter.9
where the time goes:
time: 562 us; the launch traced here: 561 us
  blocking collectives  177 us (31%)
  waiting for transfers between devices  175 us (31%)
  local copies, waits for them, and re-layouts  89.7 us (16%)
  loops' own time  63.5 us (11%)
  matrix products  21.7 us (4%)
  starting transfers between devices  15.9 us (3%)
  between operations  13.9 us (2%)
    psum x2, blocking collectives, per_device(): squares = lax.psum(jnp.sum(summed * summed, 0), ('leaf', 'mode'))  129 us
    unnamed x4, waiting for transfers between devices  82.7 us
    reduce_scatter x1, waiting for transfers between devices, per_device(): lax.psum_scatter(assemble_rows(jnp.int32(0), lax.axis_size(('leaf', 'mode...  80.6 us
    another operation x2, loops' own time, coupled_correction(): return lax.fori_loop(0, blocks.shape[0], add_slot, initial)  63.5 us
    dynamic_update_slice x48, local copies, waits for them, and re-layouts, add_slot(): lax.dynamic_update_slice_in_dim(accumulated, current + update, offset, 0)  60.6 us
    all_gather x2, blocking collectives, gather_rows(): return lax.all_gather(own_block, ('leaf', 'mode'), axis=0, tiled=True)  48 us
    dynamic_slice x32, local copies, waits for them, and re-layouts, add_slot(): offset = offsets[slot_index]  18.8 us
    dot_general x32, matrix products, add_slot(): jnp.einsum('mw,mc->wc', weights, projected, preferred_element_type=jnp.fl...  11.9 us
  transfers between devices with their start and end apart: 5, of which 4 were waited for; matrix products, arithmetic and copies ran while one was open for 1% of the time, Pallas kernels for 0%

commit v1 on v0

--- a/solution.py
+++ b/solution.py
@@ -1,3 +1,4 @@
+import functools
 import jax
 import jax.numpy as jnp
 from jax import lax
@@ -7,6 +8,15 @@
 CAP = 2
 ITERS = 2
 epsilon = 1e-06
+
+
+def find_streams(my_data, ax_name, axis_name):
+    x_next = lax.psum(my_data, axis_name=ax_name)
+    side_arr = lax.psum(x_next, axis_name=axis_name)
+    return side_arr
+
+
+_group_stages_all = functools.partial(find_streams, ax_name="mode", axis_name="leaf")
 
 
 def leaf_projection(modes, coupling, eigenvalues):
@@ -93,7 +103,7 @@
             scatter_dimension=0,
             tiled=True,
         )
-        squares = lax.psum(jnp.sum(summed * summed, 0), ("leaf", "mode"))
+        squares = _group_stages_all(jnp.sum(summed * summed, 0))
         column_scale = jnp.sqrt(squares / SEP_ROWS + epsilon)
         normed = (summed / column_scale).astype(jnp.bfloat16)
         own_block = jnp.dot(

time: 562 us -> 517 us (0.920); the launches traced: 561 us -> 509 us
  blocking collectives: 177 us -> 126 us
    psum x2 -> x4, blocking collectives: 129 us -> 70.8 us  [the longest x2 61.7 us: find_streams(): side_arr = lax.psum(x_next, axis_name=axis_name)]
    all_gather x2, blocking collectives: 48 us -> 54.7 us  [gather_rows(): return lax.all_gather(own_block, ('leaf', 'mode'), axis=0, tiled=True)]
where the time goes in v1:
time: 517 us; the launch traced here: 509 us
  waiting for transfers between devices  175 us (34%)
  blocking collectives  126 us (24%)
  local copies, waits for them, and re-layouts  89.7 us (17%)
  loops' own time  63.5 us (12%)
  matrix products  21.7 us (4%)
  starting transfers between devices  15.9 us (3%)
  between operations  13.9 us (3%)
    unnamed x4, waiting for transfers between devices  82.9 us
    reduce_scatter x1, waiting for transfers between devices, per_device(): lax.psum_scatter(assemble_rows(jnp.int32(0), lax.axis_size(('leaf', 'mode...  80.6 us
    another operation x2, loops' own time, coupled_correction(): return lax.fori_loop(0, blocks.shape[0], add_slot, initial)  63.5 us
    psum x2, blocking collectives, find_streams(): side_arr = lax.psum(x_next, axis_name=axis_name)  61.7 us
    dynamic_update_slice x48, local copies, waits for them, and re-layouts, add_slot(): lax.dynamic_update_slice_in_dim(accumulated, current + update, offset, 0)  60.6 us
    all_gather x2, blocking collectives, gather_rows(): return lax.all_gather(own_block, ('leaf', 'mode'), axis=0, tiled=True)  54.7 us
    dynamic_slice x32, local copies, waits for them, and re-layouts, add_slot(): offset = offsets[slot_index]  18.8 us
    dot_general x32, matrix products, add_slot(): jnp.einsum('mw,mc->wc', weights, projected, preferred_element_type=jnp.fl...  11.9 us
  transfers between devices with their start and end apart: 5, of which 4 were waited for; matrix products, arithmetic and copies ran while one was open for 1% of the time, Pallas kernels for 0%

profile of v1, /device:TPU:1, one launch (start us, length us, event | category | flops | bytes accessed | tf_op | source)
XLA Modules:
  0.0 509.4 jit_solution(4798464849297094999)
XLA Ops:
  7.3 6.2 %convolution_bitcast_fusion = f32[256,8,256]{0,2,1:T(8,128)} fusion(bf16[8,1024,256]{2,1,0:T(8,128)(2,1)} %param.13, bf16[8,1024,256]{2,1,0:T(8,128)(2,1)} %param.12), kind=kOutput, calls=%fused_computation.13 | convolution fusion | flops 1073741824 | bytes 10485760 | tf_op jit(solution)/shard_map/ldm,ldw->mlw/dot_general | solution.py:24
  14.5 9.0 %all-to-all-start = ((s32[8,1,2]{2,1,0:T(1,128)}), s32[8,1,2]{2,1,0:T(1,128)S(1)}, u32[]{:S(2)}, u32[]{:S(2)}) async-start(s32[8,1,2]{2,1,0:T(1,128)} %bitcast.7), calls=%async_computation | async-start | bytes 8192 | tf_op jit(solution)/shard_map/all_to_all | solution.py:50
  23.5 9.3 %reduce-scatter.6.cloned.1.call-done = f32[128,8,256]{0,2,1:T(8,128)} async-done(((f32[256,8,256]{0,2,1:T(8,128)}), f32[128,8,256]{0,2,1:T(8,128)}) %reduce-scatter.6.cloned.1.call-update) | async-done | bytes 1048592 | tf_op jit(solution)/shard_map/reduce_scatter | solution.py:23
  37.3 6.8 %all-to-all-start.1 = ((bf16[8,2,128,256]{3,1,2,0:T(2,128)(2,1)}), bf16[8,2,128,256]{3,1,2,0:T(2,128)(2,1)S(1)}, u32[]{:S(2)}, u32[]{:S(2)}) async-start(bf16[8,2,128,256]{3,1,2,0:T(2,128)(2,1)} %copy.30), calls=%async_computation.2 | async-start | bytes 2097152 | tf_op jit(solution)/shard_map/all_to_all | solution.py:47
  44.2 25.3 %all-gather = bf16[1,512,256]{2,1,0:T(8,128)(2,1)S(1)} all-gather(bf16[1,16,256]{2,1,0:T(8,128)(2,1)S(1)} %copy-done.1), channel_id=2, replica_groups=mesh['leaf'=16,'sep'=8,'mode'=2] {'leaf','mode'}, dimensions={1}, use_global_device_ids=true | all-gather | bytes 270336 | tf_op jit(solution)/shard_map/all_gather | solution.py:79
  70.8 2.6 all-to-all-done.1
  73.6 74.0 %while.26 = (s32[]{:T(128)}, f32[512,256]{1,0:T(8,128)S(1)}, s32[16]{0:T(128)S(1)}, bf16[16,128,256]{2,1,0:T(8,128)(2,1)S(1)}, bf16[512,256]{1,0:T(8,128)(2,1)S(1)}, /*index=5*/s32[]{:T(128)}, s32[]{:T(128)}, s32[]{:T(128)}) while((s32[]{:T(128)}, f32[512,256]{1,0:T(8,128)S(1)}, s32[16]{0:T(128)S(1)}, bf16[16,128,256]{2,1,0:T(8,128)(2,1)S(1)}, ...), condition=%wide.region_4.5_spmd, body=%wide.region_3.4_spmd.sunk | while | flops 33652740 | bytes 1312903 | solution.py:75
  148.8 80.6 %reduce-scatter.8.cloned.1.call-done = f32[16,256]{1,0:T(8,128)} async-done(((f32[512,256]{1,0:T(8,128)}), f32[16,256]{1,0:T(8,128)}) %reduce-scatter.8.cloned.1.call-update) | async-done | bytes 16400 | tf_op jit(solution)/shard_map/reduce_scatter | solution.py:100
  230.1 4.7 psum.28
  234.8 30.8 %psum.29 = f32[256]{0:T(256)S(1)} all-reduce(f32[256]{0:T(256)S(1)} %psum.28), channel_id=1, replica_groups=mesh['leaf'=16,'sep'=8,'mode'=2] {'leaf'}, use_global_device_ids=true, to_apply=%region_8.9 | all-reduce | flops 256 | bytes 2048 | tf_op jit(solution)/shard_map/psum | solution.py:15
  266.5 29.4 %all_gather.7 = bf16[512,256]{1,0:T(8,128)(2,1)S(1)} all-gather(bf16[16,256]{1,0:T(8,128)(2,1)S(1)} %convolution_convert_fusion.4), channel_id=1, replica_groups=mesh['leaf'=16,'sep'=8,'mode'=2] {'leaf','mode'}, dimensions={0}, use_global_device_ids=true | all-gather | bytes 270336 | tf_op jit(solution)/shard_map/all_gather | solution.py:79
  295.9 85.1 %while.27 = (s32[]{:T(128)}, f32[512,256]{0,1:T(8,128)S(1)}, s32[16]{0:T(128)S(1)}, bf16[16,128,256]{2,1,0:T(8,128)(2,1)S(1)}, bf16[512,256]{1,0:T(8,128)(2,1)S(1)}, /*index=5*/s32[]{:T(128)}, s32[]{:T(128)}, s32[]{:T(128)}) while((s32[]{:T(128)}, f32[512,256]{0,1:T(8,128)S(1)}, s32[16]{0:T(128)S(1)}, bf16[16,128,256]{2,1,0:T(8,128)(2,1)S(1)}, ...), condition=%wide.region_10.11_spmd, body=%wide.region_9.10_spmd.sunk | while | flops 33652740 | bytes 2884751 | solution.py:75
  304.5 1.9 dynamic_update_slice.17
  309.8 1.9 dynamic_update_slice.17
  315.0 1.9 dynamic_update_slice.17
  330.8 2.2 dynamic_update_slice.17
  336.4 1.9 dynamic_update_slice.17
  346.9 1.9 dynamic_update_slice.17
  352.2 2.2 dynamic_update_slice.17
  357.8 1.9 dynamic_update_slice.17
  373.5 2.2 dynamic_update_slice.17
  382.3 82.8 %reduce-scatter.10.cloned.1.call-done = f32[16,256]{1,0:T(8,128)} async-done(((f32[512,256]{1,0:T(8,128)}), f32[16,256]{1,0:T(8,128)}) %reduce-scatter.10.cloned.1.call-update) | async-done | bytes 16400
  466.1 4.5 psum.30
  470.6 30.8 %psum.31 = f32[256]{0:T(256)S(1)} all-reduce(f32[256]{0:T(256)S(1)} %psum.30), channel_id=1, replica_groups=mesh['leaf'=16,'sep'=8,'mode'=2] {'leaf'}, use_global_device_ids=true, to_apply=%region_14.15 | all-reduce | flops 256 | bytes 2048 | tf_op jit(solution)/shard_map/psum | solution.py:15
  (181 shorter events, 90.8 us)
Async XLA Ops:
  7.2 140.5 %copy-start = (bf16[1,512,16]{1,2,0:T(8,128)(2,1)S(1)}, bf16[1,512,16]{1,2,0:T(8,128)(2,1)}, u32[]{:S(2)}) copy-start(bf16[1,512,16]{1,2,0:T(8,128)(2,1)} %param.17) | copy-start | bytes 49156
  7.2 6.3 %copy-start.4 = (s32[8,1]{0,1:T(1,128)S(1)}, s32[8,1]{0,1:T(1,128)}, u32[]{:S(2)}) copy-start(s32[8,1]{0,1:T(1,128)} %param.15) | copy-start | bytes 100
  7.2 6.5 %copy-start.5 = (s32[8]{0:T(128)S(1)}, s32[8]{0:T(128)}, u32[]{:S(2)}) copy-start(s32[8]{0:T(128)} %param.16) | copy-start | bytes 100
  7.2 16.3 %copy-start.2 = (f32[8,128]{1,0:T(8,128)S(1)}, f32[8,128]{1,0:T(8,128)}, u32[]{:S(2)}) copy-start(f32[8,128]{1,0:T(8,128)} %param.14) | copy-start | bytes 12292
  7.2 25.6 %reduce-scatter.6.cloned.1.call-start = ((), (), s32[]{:S(2)}) async-start(), calls=%async_computation.5 | async-start | bytes 3145728 | tf_op jit(solution)/shard_map/reduce_scatter | solution.py:23
  14.5 22.9 %all-to-all-start = ((s32[8,1,2]{2,1,0:T(1,128)}), s32[8,1,2]{2,1,0:T(1,128)S(1)}, u32[]{:S(2)}, u32[]{:S(2)}) async-start(s32[8,1,2]{2,1,0:T(1,128)} %bitcast.7), calls=%async_computation | async-start | bytes 8192 | tf_op jit(solution)/shard_map/all_to_all | solution.py:50
  34.5 9.6 %copy-start.1 = (bf16[1,16,256]{2,1,0:T(8,128)(2,1)S(1)}, bf16[1,16,256]{2,1,0:T(8,128)(2,1)}, u32[]{:S(2)}) copy-start(bf16[1,16,256]{2,1,0:T(8,128)(2,1)} %param.18) | copy-start | bytes 24580
  37.3 36.0 %all-to-all-start.1 = ((bf16[8,2,128,256]{3,1,2,0:T(2,128)(2,1)}), bf16[8,2,128,256]{3,1,2,0:T(2,128)(2,1)S(1)}, u32[]{:S(2)}, u32[]{:S(2)}) async-start(bf16[8,2,128,256]{3,1,2,0:T(2,128)(2,1)} %copy.30), calls=%async_computation.2 | async-start | bytes 2097152 | tf_op jit(solution)/shard_map/all_to_all | solution.py:47
  44.1 185.3 %reduce-scatter.8.cloned.1.call-start = ((), (), s32[]{:S(2)}) async-start(), calls=%async_computation.6 | async-start | bytes 540672 | tf_op jit(solution)/shard_map/reduce_scatter | solution.py:100
  73.6 192.1 %copy-start.3 = (bf16[1,2,256,256]{3,2,1,0:T(8,128)(2,1)S(1)}, bf16[1,2,256,256]{3,2,1,0:T(8,128)(2,1)}, u32[]{:S(2)}) copy-start(bf16[1,2,256,256]{3,2,1,0:T(8,128)(2,1)} %param.19) | copy-start | bytes 786436
  148.7 316.4 %reduce-scatter.10.cloned.1.call-start = ((), (), s32[]{:S(2)}) async-start(), calls=%async_computation.7 | async-start | bytes 540672
Sparse Core Ops, SparseCore 0:
  13.6 19.1 reduce-scatter.5
  148.9 80.5 reduce-scatter.7
  382.4 82.6 reduce-scatter.9
